TPU v7x, 128 devices: a whole 4x4x4 slice. The times are simulated.
128 devices in a mesh: lat: 8 (over y_lo, x), lon: 16 (over z, y_hi, core).
Axes of the slice: x: 4, y: 4 (y_hi: 2, y_lo: 2; y = y_hi * 2 + y_lo), z: 4, core: 2. Of those that a mesh axis runs over, the one named last changes fastest.
Arguments:
- block_input: float32 [192, 384, 384], P('lat', 'lon'), may hold values from -90 to 90, as said below
- cotangent: float32 [192, 384, 384], P('lat', 'lon'), may hold values from -6 to 6
- weights: float32 [1769472], replicated, may hold values from -4 to 4, as said below
- first_moment: float32 [1769472], P(('lat', 'lon')), may hold values from -3 to 3
- second_moment: float32 [1769472], P(('lat', 'lon')), may hold values from 0.05 to 2
- bias_table: float32 [12, 529], replicated, may hold values from -5 to 5
- bias_index: int32 [144, 144], replicated, may hold values from 0 to 528
- region_ids: int32 [192, 384], P('lat', 'lon'), may hold values from 0 to 2
Outputs:
- grad_input: float32 [192, 384, 384], P('lat', 'lon')
- weights_new: float32 [1769472], replicated
- first_new: float32 [1769472], P(('lat', 'lon'))
- second_new: float32 [1769472], P(('lat', 'lon'))
- table_grad: float32 [12, 529], replicated
Inputs may be any that keep to these rules, and one draw needn't show every extreme that they name: `block_input`: Tokens' features; real values. `weights`: real values. `region_ids`: entry (r, c) is the region of the token at ((r + 6) mod 192, (c + 6) mod 384) of the input grid.
All inputs are finite; a program needn't handle non-finite values.
Results may differ from a plain program's by a relative error of at most 0.0003.
Values sent between devices are 32-bit elements; how exact they have to be, the bound alone decides.
No kernel may reach another device: no remote copies, remote signals or barrier semaphores. Data moves between devices by JAX's collectives and lax.ppermute only.
A program may use at most 128 MiB of HBM per device.

v0:
```python
import math
import jax
import jax.numpy as jnp
from jax import lax
from jax.sharding import PartitionSpec as P

D = 384
HEADS = 12
FF = 1536
WIN = 12
HEAD_DIM = 32
SHIFT = 6
precise = lax.Precision.HIGHEST


def passed_along(value, axis, by):
    size = lax.axis_size(axis)
    return lax.ppermute(value, axis, [(i, (i + by) % size) for i in range(size)])


def split_up(value, dim, size):
    before, after = (value.shape[:dim], value.shape[dim + 1 :])
    return jnp.moveaxis(value.reshape(*before, size, -1, *after), dim, 0)


def sent_and_summed(value, axis, dim):
    blocks = split_up(value, dim, lax.axis_size(axis))
    arrived = lax.all_to_all(blocks, axis, split_axis=0, concat_axis=0, tiled=True)
    return arrived.sum(axis=0)


def laid_out(blocks, dim):
    blocks = jnp.moveaxis(blocks, 0, dim)
    dims = blocks.shape
    return blocks.reshape(*dims[:dim], dims[dim] * dims[dim + 1], *dims[dim + 2 :])


def copy_for_each(value, axis):
    copies = jnp.broadcast_to(value, (lax.axis_size(axis), *value.shape))
    return lax.all_to_all(copies, axis, split_axis=0, concat_axis=0, tiled=True)


def collect(value, axis, dim):
    return laid_out(copy_for_each(value, axis), dim)


def normalize(values):
    center = values - jnp.mean(values, axis=-1, keepdims=True)
    spread = jnp.mean(center * center, axis=-1, keepdims=True)
    return center / jnp.sqrt(spread + 1e-05)


def windows(tensor):
    height, breadth, features = tensor.shape
    blocks = tensor.reshape(height // WIN, WIN, breadth // WIN, WIN, features)
    return blocks.transpose(0, 2, 1, 3, 4).reshape(-1, WIN * WIN, features)


def unwindow(blocks, height, breadth):
    features = blocks.shape[-1]
    tensor = blocks.reshape(height // WIN, breadth // WIN, WIN, WIN, features)
    return tensor.transpose(0, 2, 1, 3, 4).reshape(height, breadth, features)


def unpack(packed):
    first_cut = D * 3 * D
    second_cut = first_cut + D * D
    third_cut = second_cut + D * FF
    return (
        packed[:first_cut].reshape(D, 3 * D),
        packed[first_cut:second_cut].reshape(D, D),
        packed[second_cut:third_cut].reshape(D, FF),
        packed[third_cut:].reshape(FF, D),
    )


def attend(tensor, w_all, bias_table, bias_index, region_ids, wrapped):
    w_qkv, w_proj, _, _ = unpack(w_all)
    height, breadth, _ = tensor.shape
    flat_rows = normalize(tensor).reshape(-1, D)
    mixed = jnp.dot(flat_rows, w_qkv, precision=precise, preferred_element_type=jnp.float32)
    mixed = windows(mixed.reshape(height, breadth, 3 * D))
    window_count = mixed.shape[0]
    query = mixed[:, :, :D].reshape(window_count, WIN * WIN, HEADS, HEAD_DIM)
    keyed = mixed[:, :, D : 2 * D].reshape(window_count, WIN * WIN, HEADS, HEAD_DIM)
    valued = mixed[:, :, 2 * D :].reshape(window_count, WIN * WIN, HEADS, HEAD_DIM)
    scores = jnp.einsum("wihd,wjhd->whij", query, keyed, precision=precise) / math.sqrt(HEAD_DIM)
    scores = scores + jnp.take(bias_table, bias_index, axis=1)[None]
    labels = windows(region_ids[:, :, None])[:, :, 0]
    halves = windows(
        jnp.broadcast_to(wrapped[:, None, None], (height, breadth, 1)).astype(jnp.int32)
    )[:, :, 0]
    allowed = (labels[:, :, None] == labels[:, None, :]) & (
        halves[:, :, None] == halves[:, None, :]
    )
    allowed = allowed[:, None]
    masked = jnp.where(allowed, scores, -jnp.inf)
    summit = lax.stop_gradient(jnp.max(masked, axis=-1, keepdims=True))
    raised = jnp.exp(masked - summit)
    probability = raised / jnp.sum(raised, axis=-1, keepdims=True)
    context = jnp.einsum("whij,wjhd->wihd", probability, valued, precision=precise)
    context = unwindow(context.reshape(window_count, WIN * WIN, D), height, breadth).reshape(-1, D)
    return jnp.dot(context, w_proj, precision=precise, preferred_element_type=jnp.float32).reshape(
        height, breadth, D
    )


def feed(tensor, w_all):
    _, _, w_up, w_down = unpack(w_all)
    flat_rows = normalize(tensor).reshape(-1, D)
    hidden = jax.nn.gelu(
        jnp.dot(flat_rows, w_up, precision=precise, preferred_element_type=jnp.float32),
        approximate=True,
    )
    return jnp.dot(hidden, w_down, precision=precise, preferred_element_type=jnp.float32).reshape(
        tensor.shape
    )


def shift_ahead(stacked):
    from_east = passed_along(stacked[:, :, :SHIFT], "lon", -1)
    widened = jnp.concatenate([stacked[:, :, SHIFT:], from_east], axis=2)
    from_south = passed_along(widened[:, :SHIFT], "lat", -1)
    return jnp.concatenate([widened[:, SHIFT:], from_south], axis=1)


def shift_back(stacked):
    from_north = passed_along(stacked[:, -SHIFT:], "lat", 1)
    lengthened = jnp.concatenate([from_north, stacked[:, :-SHIFT]], axis=1)
    from_west = passed_along(lengthened[:, :, -SHIFT:], "lon", 1)
    return jnp.concatenate([from_west, lengthened[:, :, :-SHIFT]], axis=2)


def per_device(
    block_input, cotangent, weights, first_moment, second_moment, bias_table, bias_index, region_ids
):
    tile_rows, tile_cols, _ = block_input.shape
    lat_count = lax.axis_size("lat")
    lon_count = lax.axis_size("lon")
    global_rows = lax.axis_index("lat") * tile_rows + jnp.arange(tile_rows)
    wrapped = global_rows >= tile_rows * lat_count - SHIFT

    def attention_part(tensor, w_all, table):
        return attend(tensor, w_all, table, bias_index, region_ids, wrapped)

    shifted = shift_ahead(block_input[None])[0]
    attn_shifted, pull_attn = jax.vjp(attention_part, shifted, weights, bias_table)
    mixed = block_input + shift_back(attn_shifted[None])[0]
    _, pull_feed = jax.vjp(feed, mixed, weights)
    grad_feed, weights_feed = pull_feed(cotangent)
    grad_mixed = cotangent + grad_feed
    grad_moved = shift_ahead(grad_mixed[None])[0]
    grad_shifted, weights_attn, grad_table = pull_attn(grad_moved)
    grad_input = grad_mixed + shift_back(grad_shifted[None])[0]
    grad_weights = weights_feed + weights_attn
    factor = 1.0 / math.sqrt(tile_rows * tile_cols * lat_count * lon_count)
    shard_len = first_moment.shape[0]
    partial_sum = sent_and_summed(grad_weights, "lat", 0)
    summed = sent_and_summed(partial_sum, "lon", 0) * factor
    owner_rank = lax.axis_index("lat") * lon_count + lax.axis_index("lon")
    own_weights = lax.dynamic_slice_in_dim(weights, owner_rank * shard_len, shard_len)
    first_new = 0.9 * first_moment + 0.1 * summed
    second_new = 0.95 * second_moment + 0.05 * summed * summed
    own_new = own_weights - 0.01 * first_new / (jnp.sqrt(second_new) + 1e-08)
    along_lon = collect(own_new, "lon", 0)
    gathered = lax.all_gather(along_lon, "lat", axis=0, tiled=True)
    table_grad = lax.psum(grad_table, ("lat", "lon")) * factor
    return (grad_input, gathered, first_new, second_new, table_grad)


def solution(mesh):
    placed = (
        P("lat", "lon", None),
        P("lat", "lon", None),
        P(),
        P(("lat", "lon")),
        P(("lat", "lon")),
        P(),
        P(),
        P("lat", "lon"),
    )
    return jax.shard_map(
        per_device,
        mesh=mesh,
        in_specs=placed,
        out_specs=(P("lat", "lon", None), P(), P(("lat", "lon")), P(("lat", "lon")), P()),
        check_vma=False,
    )
```

profile of v0, /device:TPU:0, one launch (start us, length us, event | category | flops | bytes accessed | tf_op | source)
XLA Modules:
  0.0 694.5 jit_solution(7623276320993546166)
XLA Ops:
  8.2 6.3 collective-permute-start
  19.8 38.8 %gather_fusion = f32[20736,12]{1,0:T(8,128)} fusion(f32[12,529]{0,1:T(8,128)S(1)} %copy.129, s32[21504]{0:T(1024)S(1)} %pad_clamp_fusion), kind=kCustom, calls=%fused_computation | custom fusion | bytes 2073600 | tf_op jit(solution)/shard_map/jvp(jit(_take))/gather | solution.py:88
  58.5 12.1 %copy.130 = f32[144,144,12]{0,1,2:T(8,128)} copy(f32[144,144,12]{2,1,0:T(8,128)} %bitcast.115) | data formatting | bytes 1990656 | tf_op jit(solution)/shard_map/jvp(jit(_take))/gather | solution.py:88
  92.5 8.2 %convolution_bitcast_fusion = f32[2,2,12,12,1152]{4,3,1,2,0:T(8,128)S(1)} fusion(f32[384,1152,1,1,1]{1,0,2,3,4:T(8,128)} %reshape.392, f32[2,12,2,12,384]{4,3,2,1,0:T(8,128)} %squeeze.11, f32[2,12,2,12]{3,2,1,0:T(2,128)S(1)} %sqrt.38, f32[2,12,2,12]{3,2,1,0:T(2,128)S(1)} %div.137), kind=kOutput, calls=%fused_computation.14 | convolution fusion | flops 3058089984 | bytes 5313024 | tf_op jit(solution)/shard_map/jvp()/dot_general | solution.py:81
  103.6 4.9 reshape.353
  119.0 9.5 %fusion.4 = (f32[4,12,144]{2,1,0:T(8,128)S(1)}, f32[4,12,144,144]{2,3,1,0:T(8,128)S(1)}) fusion(f32[12,144,144]{1,2,0:T(8,128)S(1)} %select_bitcast_fusion, pred[4,144,144]{1,2,0:T(8,128)(4,1)S(1)} %copy-done.23, f32[4,144,12,32]{1,3,2,0:T(8,128)} %bitcast.118, f32[4,144,12,32]{1,3,2,0:T(8,128)} %bitcast.116), kind=kOutput, calls=%fused_computation.11 | convolution fusion | flops 386180352 | bytes 6856704 | tf_op jit(solution)/shard_map/jvp(wihd,wjhd->whij)/dot_general | solution.py:87
  131.5 7.0 %fusion.25 = f32[4,144,12,32]{1,3,2,0:T(8,128)} fusion(f32[4,144,12,32]{1,3,2,0:T(8,128)S(1)} %bitcast.129, f32[4,12,144]{2,1,0:T(8,128)S(1)} %fusion.52, f32[4,12,144,144]{2,3,1,0:T(8,128)S(1)} %get-tuple-element.56, f32[4,12,144]{2,1,0:T(8,128)S(1)} %get-tuple-element.55, f32[12,144,144]{1,2,0:T(8,128)S(1)} %select_bitcast_fusion, ...), kind=kOutput, calls=%fused_computation.37 | convolution fusion | flops 387182592 | bytes 6884352 | tf_op jit(solution)/shard_map/jvp(whij,wjhd->wihd)/dot_general | solution.py:101
  138.5 6.2 copy.132
  170.3 9.1 %collective-permute-done.3 = f32[1,24,6,384]{3,2,1,0:T(8,128)S(1)} collective-permute-done((f32[1,24,6,384]{3,2,1,0:T(8,128)S(1)}, f32[1,24,6,384]{3,2,1,0:T(8,128)S(1)}, u32[]{:S(2)}, u32[]{:S(2)}) %collective-permute-start.3) | collective-permute-done | bytes 221216 | tf_op jit(solution)/shard_map/ppermute | solution.py:18
  180.2 5.9 fusion.59
  186.1 7.9 %fusion.10 = f32[576,1536]{1,0:T(8,128)S(1)} fusion(f32[576,1536]{1,0:T(8,128)S(1)} %fusion.59, f32[576,384]{1,0:T(8,128)S(1)} %bitcast.134, f32[1536,384]{1,0:T(8,128)S(1)} %copy-done.28), kind=kOutput, calls=%fused_computation.20 | convolution fusion | flops 4093673472 | bytes 10321920 | tf_op jit(solution)/shard_map/transpose(jvp())/dot_general | solution.py:115
  194.0 5.8 multiply_reduce_fusion.2
  201.2 9.7 %fusion.11 = f32[1536,384]{1,0:T(8,128)} fusion(f32[576,384]{1,0:T(8,128)S(1)} %bitcast.135, f32[576,1536]{1,0:T(8,128)S(1)} %fusion.59), kind=kOutput, calls=%fused_computation.21 | convolution fusion | flops 4083941376 | bytes 6782976 | tf_op jit(solution)/shard_map/transpose(jvp())/dot_general | solution.py:115
  212.0 4.5 collective-permute-start.5
  216.5 5.9 fusion.60
  239.3 5.7 copy.135
  245.0 13.7 %fusion.17 = f32[4,12,32,144]{3,2,1,0:T(8,128)} fusion(f32[4,12,32,144]{3,2,1,0:T(8,128)} %copy.135, f32[4,12,144]{2,1,0:T(8,128)} %copy-done.37, f32[4,12,144,144]{2,3,1,0:T(8,128)} %copy-done, f32[4,12,144]{2,1,0:T(8,128)} %copy-done.33, f32[12,144,144]{1,2,0:T(8,128)} %copy-done.1, pred[4,144,144]{1,2,0:T(8,128)(4,1)} %compare_and_fusion), kind=kOutput, calls=%fused_computation.28 | convolution fusion | flops 387182592 | bytes 6884352 | tf_op jit(solution)/shard_map/transpose(jvp(whij,wjhd->wihd))/dot_general | solution.py:101
  258.9 9.2 %multiply_reduce_fusion = (f32[4,12,144]{2,1,0:T(8,128)S(1)}, f32[4,12,144,144]{2,3,1,0:T(8,128)S(1)}) fusion(f32[4,12,144]{2,1,0:T(8,128)S(1)} %copy-done.42, f32[4,12,144]{2,1,0:T(8,128)S(1)} %copy-done.34, f32[12,144,144]{1,2,0:T(8,128)S(1)} %copy-done.2, f32[4,12,144,144]{2,3,1,0:T(8,128)S(1)} %bitcast.112, pred[4,144,144]{1,2,0:T(8,128)(4,1)S(1)} %copy-done.24, ...), kind=kOutput, calls=%fused_computation.4 | convolution fusion | flops 389166336 | bytes 10893312 | tf_op jit(solution)/shard_map/transpose(jvp(whij,wjhd->wihd))/dot_general | solution.py:101
  268.1 5.0 fusion.53
  277.3 8.6 %fusion.2 = f32[4,12,144,32]{2,3,1,0:T(8,128)} fusion(f32[4,144,12,32]{1,3,2,0:T(8,128)S(1)} %bitcast.119, f32[4,12,144,144]{2,3,1,0:T(8,128)S(1)} %get-tuple-element.36), kind=kOutput, calls=%fused_computation.9 | convolution fusion | flops 383201280 | bytes 5750784 | tf_op jit(solution)/shard_map/transpose(jvp(wihd,wjhd->whij))/dot_general | solution.py:87
  309.6 7.0 %fusion.62 = f32[384,1152]{1,0:T(8,128)} fusion(f32[576,384]{1,0:T(8,128)} %bitcast.138, f32[576,1152]{1,0:T(8,128)S(1)} %reshape.369), kind=kOutput, calls=%fused_computation.119 | convolution fusion | flops 3057647616 | bytes 5308416 | tf_op jit(solution)/shard_map/transpose(jvp())/dot_general | solution.py:81
  319.3 9.8 %add_add_fusion = f32[1769472]{0:T(1024)S(1)} fusion(f32[442368]{0:T(1024)} %reshape.370, f32[147456]{0:T(1024)} %reshape.368, f32[589824]{0:T(1024)} %reshape.366, f32[589824]{0:T(1024)S(1)} %copy-done.9), kind=kLoop, calls=%fused_computation.2 | loop fusion | flops 5308416 | bytes 14155776 | tf_op jit(solution)/shard_map/add | solution.py:155
  329.0 84.6 %all_to_all.24 = f32[8,1,221184]{2,1,0:T(1,128)} all-to-all(f32[8,1,221184]{2,1,0:T(1,128)S(1)} %bitcast.113), channel_id=1, replica_groups=mesh['lat'=8,'lon'=16] {'lat'}, dimensions={0} | all-to-all | bytes 14155776 | tf_op jit(solution)/shard_map/all_to_all | solution.py:28
  413.6 10.5 %reduce_sum.132 = f32[221184]{0:T(1024)} reduce(f32[8,1,221184]{2,1,0:T(1,128)} %all_to_all.24, f32[]{:T(128)} %constant.31.clone.1), dimensions={0,1}, to_apply=%region_11.12 | reduce | flops 1548288 | bytes 7962628 | tf_op jit(solution)/shard_map/reduce_sum | solution.py:29
  427.9 16.1 %all-to-all-done.1 = f32[16,1,13824]{2,1,0:T(1,128)S(1)} async-done(((f32[16,1,13824]{2,1,0:T(1,128)}), f32[16,1,13824]{2,1,0:T(1,128)S(1)}, u32[]{:S(2)}, u32[]{:S(2)}) %all-to-all-start.1) | async-done | bytes 884768 | tf_op jit(solution)/shard_map/all_to_all | solution.py:28
  446.6 19.5 %all_to_all.25 = f32[16,1,13824]{2,1,0:T(1,128)} all-to-all(f32[16,1,13824]{2,1,0:T(1,128)S(1)} %broadcast_in_dim.93), channel_id=1, replica_groups=mesh['lat'=8,'lon'=16] {'lon'}, dimensions={0} | all-to-all | bytes 1769472 | tf_op jit(solution)/shard_map/all_to_all | solution.py:40
  470.7 6.3 multiply_reduce_fusion.1
  481.7 10.4 %copy.157 = f32[144,144,12]{2,1,0:T(8,128)} copy(f32[144,144,12]{0,1,2:T(8,128)S(1)} %bitcast.126) | data formatting | bytes 1990656 | tf_op jit(solution)/shard_map/transpose(jvp())/reduce_sum | solution.py:88
  492.1 112.5 %scatter_custom_fusion = f32[12,529]{0,1:T(8,128)S(1)} fusion(s32[20736]{0:T(1024)} %copy-done.39, f32[20736,12]{1,0:T(8,128)} %bitcast.121, f32[]{:T(128)} %constant.31.clone.1), kind=kCustom, calls=%fused_computation.81 | custom fusion | flops 248832 | bytes 25904 | tf_op jit(solution)/shard_map/transpose(jvp(jit(_take)))/scatter-add | solution.py:88
  604.6 65.4 %psum.7 = f32[12,529]{0,1:T(8,128)S(1)} all-reduce(f32[12,529]{0,1:T(8,128)S(1)} %scatter_custom_fusion), channel_id=1, replica_groups=mesh['lat'=8,'lon'=16] {'lat','lon'}, use_global_device_ids=true, to_apply=%region_15.16 | all-reduce | flops 6348 | bytes 50784 | tf_op jit(solution)/shard_map/psum | solution.py:167
  670.9 8.9 %collective-permute-done.7 = f32[1,24,6,384]{3,2,1,0:T(8,128)S(1)} collective-permute-done((f32[1,24,6,384]{3,2,1,0:T(8,128)S(1)}, f32[1,24,6,384]{3,2,1,0:T(8,128)S(1)}, u32[]{:S(2)}, u32[]{:S(2)}) %collective-permute-start.7) | collective-permute-done | bytes 221216 | tf_op jit(solution)/shard_map/ppermute | solution.py:18
  682.2 5.2 copy.164
  (220 shorter events, 139.2 us)
Async XLA Ops:
  7.2 12.4 %copy-start.50 = (f32[12,529]{1,0:T(8,128)S(1)}, f32[12,529]{1,0:T(8,128)}, u32[]{:S(2)}) copy-start(f32[12,529]{1,0:T(8,128)} %param.13) | copy-start | bytes 76180
  8.2 64.1 %collective-permute-start = (f32[1,24,6,384]{3,2,1,0:T(8,128)S(1)}, f32[1,24,6,384]{3,2,1,0:T(8,128)S(1)}, u32[]{:S(2)}, u32[]{:S(2)}) collective-permute-start(f32[1,24,6,384]{3,2,1,0:T(8,128)S(1)} %slice.139), channel_id=1, source_target_pairs={{0,15},{1,0},{2,1},{3,2},{4,3},{5,4},{6,5},{7,6},{8,7},{9,8},{10,9... | collective-permute-start | bytes 663560 | tf_op jit(solution)/shard_map/ppermute | solution.py:18
  17.6 54.8 %copy-start.12 = (f32[1,24,18,384]{3,2,1,0:T(8,128)}, f32[1,24,18,384]{3,2,1,0:T(8,128)S(1)}, u32[]{:S(2)}) copy-start(f32[1,24,18,384]{3,2,1,0:T(8,128)S(1)} %slice.138) | copy-start | bytes 1990660
  72.3 58.4 %copy-start.1 = (f32[12,144,144]{1,2,0:T(8,128)}, f32[12,144,144]{1,2,0:T(8,128)S(1)}, u32[]{:S(2)}) copy-start(f32[12,144,144]{1,2,0:T(8,128)S(1)} %select_bitcast_fusion) | copy-start | bytes 2985988
  73.1 13.0 %collective-permute-start.1 = (f32[1,6,24,384]{3,2,1,0:T(8,128)}, f32[1,6,24,384]{3,2,1,0:T(8,128)}, u32[]{:S(2)}, u32[]{:S(2)}) collective-permute-start(f32[1,6,24,384]{3,2,1,0:T(8,128)} %pad_maximum_fusion.7), channel_id=1, source_target_pairs={{0,112},{16,0},{32,16},{48,32},{64,48},{80,64},{96,80},{112,96},{1... | collective-permute-start | bytes 663560 | tf_op jit(solution)/shard_map/ppermute | solution.py:18
  87.2 13.5 %copy-start.35 = (f32[24,24]{1,0:T(8,128)}, f32[24,24]{1,0:T(8,128)S(1)}, u32[]{:S(2)}) copy-start(f32[24,24]{1,0:T(8,128)S(1)} %broadcast_multiply_fusion.2) | copy-start | bytes 6916
  88.5 12.2 %copy-start.45 = (f32[24,24]{1,0:T(8,128)}, f32[24,24]{1,0:T(8,128)S(1)}, u32[]{:S(2)}) copy-start(f32[24,24]{1,0:T(8,128)S(1)} %multiply_reduce_fusion.4) | copy-start | bytes 6916
  89.2 11.5 %copy-start.40 = (f32[24,24]{1,0:T(8,128)}, f32[24,24]{1,0:T(8,128)S(1)}, u32[]{:S(2)}) copy-start(f32[24,24]{1,0:T(8,128)S(1)} %get-tuple-element.52) | copy-start | bytes 6916
  130.7 38.9 %copy-start.37 = (f32[4,12,144]{2,1,0:T(8,128)}, f32[4,12,144]{2,1,0:T(8,128)S(1)}, u32[]{:S(2)}) copy-start(f32[4,12,144]{2,1,0:T(8,128)S(1)} %fusion.52) | copy-start | bytes 82948
  154.0 15.1 %collective-permute-start.2 = (f32[1,6,24,384]{3,2,1,0:T(8,128)}, f32[1,6,24,384]{3,2,1,0:T(8,128)S(1)}, u32[]{:S(2)}, u32[]{:S(2)}) collective-permute-start(f32[1,6,24,384]{3,2,1,0:T(8,128)} %slice.145), channel_id=1, source_target_pairs={{0,16},{16,32},{32,48},{48,64},{64,80},{80,96},{96,112},{112,0},{1... | collective-permute-start | bytes 663560 | tf_op jit(solution)/shard_map/ppermute | solution.py:18
  163.4 16.0 %copy-start.22 = (f32[24,24,384]{2,1,0:T(8,128)S(1)}, f32[24,24,384]{2,1,0:T(8,128)}, u32[]{:S(2)}) copy-start(f32[24,24,384]{2,1,0:T(8,128)} %param.8) | copy-start | bytes 2654212
  169.1 11.1 %copy-start.11 = (f32[384,1536]{1,0:T(8,128)S(1)}, f32[384,1536]{1,0:T(8,128)}, u32[]{:S(2)}) copy-start(f32[384,1536]{1,0:T(8,128)} %slice.127) | copy-start | bytes 7077892
  169.1 10.2 %collective-permute-start.3 = (f32[1,24,6,384]{3,2,1,0:T(8,128)S(1)}, f32[1,24,6,384]{3,2,1,0:T(8,128)S(1)}, u32[]{:S(2)}, u32[]{:S(2)}) collective-permute-start(f32[1,24,6,384]{3,2,1,0:T(8,128)S(1)} %pad_maximum_fusion.5), channel_id=1, source_target_pairs={{0,1},{1,2},{2,3},{3,4},{4,5},{5,6},{6,7},{7,8},{8,9},{9,10},{10,1... | collective-permute-start | bytes 663560 | tf_op jit(solution)/shard_map/ppermute | solution.py:18
  200.9 10.0 %collective-permute-start.4 = (f32[1,24,6,384]{3,2,1,0:T(8,128)S(1)}, f32[1,24,6,384]{3,2,1,0:T(8,128)S(1)}, u32[]{:S(2)}, u32[]{:S(2)}) collective-permute-start(f32[1,24,6,384]{3,2,1,0:T(8,128)S(1)} %slice.148), channel_id=1, source_target_pairs={{0,15},{1,0},{2,1},{3,2},{4,3},{5,4},{6,5},{7,6},{8,7},{9,8},{10,9... | collective-permute-start | bytes 663560 | tf_op jit(solution)/shard_map/ppermute | solution.py:18
  212.0 16.5 %collective-permute-start.5 = (f32[1,6,24,384]{3,2,1,0:T(8,128)}, f32[1,6,24,384]{3,2,1,0:T(8,128)S(1)}, u32[]{:S(2)}, u32[]{:S(2)}) collective-permute-start(f32[1,6,24,384]{3,2,1,0:T(8,128)} %pad_maximum_fusion.6), channel_id=1, source_target_pairs={{0,112},{16,0},{32,16},{48,32},{64,48},{80,64},{96,80},{112,96},{1... | collective-permute-start | bytes 663560 | tf_op jit(solution)/shard_map/ppermute | solution.py:18
  239.3 19.5 %slice-start = ((s8[7077888]{0:T(1024)(128)(4,1)}), s8[2883584]{0:T(1024)(128)(4,1)S(1)}, s32[]{:S(2)}) async-start(s8[7077888]{0:T(1024)(128)(4,1)} %bitcast.111), calls=%async_computation.4 | async-start | bytes 5767168
  245.0 13.8 %slice-start.1 = ((s8[7077888]{0:T(1024)(128)(4,1)}), s8[4194304]{0:T(1024)(128)(4,1)S(1)}, s32[]{:S(2)}) async-start(s8[7077888]{0:T(1024)(128)(4,1)} %bitcast.111), calls=%async_computation.5 | async-start | bytes 8388608
  245.0 13.8 %copy-start.2 = (f32[12,144,144]{1,2,0:T(8,128)S(1)}, f32[12,144,144]{1,2,0:T(8,128)}, u32[]{:S(2)}) copy-start(f32[12,144,144]{1,2,0:T(8,128)} %copy-done.1) | copy-start | bytes 2985988
  245.0 13.8 %copy-start.20 = (f32[4,144,384]{1,2,0:T(8,128)S(1)}, f32[4,144,384]{1,2,0:T(8,128)}, u32[]{:S(2)}) copy-start(f32[4,144,384]{1,2,0:T(8,128)} %copy.124) | copy-start | bytes 2654212
  245.0 13.8 %copy-start.21 = (f32[4,12,32,144]{3,2,1,0:T(8,128)S(1)}, f32[4,12,32,144]{3,2,1,0:T(8,128)}, u32[]{:S(2)}) copy-start(f32[4,12,32,144]{3,2,1,0:T(8,128)} %copy.135) | copy-start | bytes 2654212
  245.0 13.8 %copy-start.24 = (pred[4,144,144]{1,2,0:T(8,128)(4,1)S(1)}, pred[4,144,144]{1,2,0:T(8,128)(4,1)}, u32[]{:S(2)}) copy-start(pred[4,144,144]{1,2,0:T(8,128)(4,1)} %compare_and_fusion) | copy-start | bytes 248836
  245.0 13.8 %copy-start.34 = (f32[4,12,144]{2,1,0:T(8,128)S(1)}, f32[4,12,144]{2,1,0:T(8,128)}, u32[]{:S(2)}) copy-start(f32[4,12,144]{2,1,0:T(8,128)} %copy-done.33) | copy-start | bytes 82948
  245.0 13.8 %copy-start.42 = (f32[4,12,144]{2,1,0:T(8,128)S(1)}, f32[4,12,144]{2,1,0:T(8,128)}, u32[]{:S(2)}) copy-start(f32[4,12,144]{2,1,0:T(8,128)} %multiply_divide_fusion) | copy-start | bytes 82948
  413.6 31.0 %copy-start.47 = (f32[13824]{0:T(1024)S(1)}, f32[13824]{0:T(1024)}, u32[]{:S(2)}) copy-start(f32[13824]{0:T(1024)} %param.11) | copy-start | bytes 165892
  413.6 31.0 %copy-start.48 = (f32[13824]{0:T(1024)S(1)}, f32[13824]{0:T(1024)}, u32[]{:S(2)}) copy-start(f32[13824]{0:T(1024)} %param.12) | copy-start | bytes 165892
  424.1 42.1 %copy-start.4 = (f32[442368]{0:T(1024)S(1)}, f32[442368]{0:T(1024)}, u32[]{:S(2)}) copy-start(f32[442368]{0:T(1024)} %copy-done.3) | copy-start | bytes 5308420
  424.1 20.0 %all-to-all-start.1 = ((f32[16,1,13824]{2,1,0:T(1,128)}), f32[16,1,13824]{2,1,0:T(1,128)S(1)}, u32[]{:S(2)}, u32[]{:S(2)}) async-start(f32[16,1,13824]{2,1,0:T(1,128)} %bitcast.136), calls=%async_computation.1 | async-start | bytes 1769472 | tf_op jit(solution)/shard_map/all_to_all | solution.py:28
  427.9 254.3 %all-gather.2.cloned.1.call-start = ((), (), s32[]{:S(2)}) async-start(), calls=%async_computation.3 | async-start | bytes 7962624 | tf_op jit(solution)/shard_map/all_gather | solution.py:166
  480.5 189.5 %collective-permute-start.6 = (f32[1,6,24,384]{3,2,1,0:T(8,128)}, f32[1,6,24,384]{3,2,1,0:T(8,128)S(1)}, u32[]{:S(2)}, u32[]{:S(2)}) collective-permute-start(f32[1,6,24,384]{3,2,1,0:T(8,128)} %slice.151), channel_id=1, source_target_pairs={{0,16},{16,32},{32,48},{48,64},{64,80},{80,96},{96,112},{112,0},{1... | collective-permute-start | bytes 663560 | tf_op jit(solution)/shard_map/ppermute | solution.py:18
  481.7 198.1 %copy-start.17 = (f32[24,24,384]{2,1,0:T(8,128)S(1)}, f32[24,24,384]{2,1,0:T(8,128)}, u32[]{:S(2)}) copy-start(f32[24,24,384]{2,1,0:T(8,128)} %copy-done.16) | copy-start | bytes 2654212
  481.7 198.1 %copy-start.44 = (f32[24,24]{1,0:T(8,128)S(1)}, f32[24,24]{1,0:T(8,128)}, u32[]{:S(2)}) copy-start(f32[24,24]{1,0:T(8,128)} %copy-done.43) | copy-start | bytes 6916
  670.0 9.8 %collective-permute-start.7 = (f32[1,24,6,384]{3,2,1,0:T(8,128)S(1)}, f32[1,24,6,384]{3,2,1,0:T(8,128)S(1)}, u32[]{:S(2)}, u32[]{:S(2)}) collective-permute-start(f32[1,24,6,384]{3,2,1,0:T(8,128)S(1)} %pad_maximum_fusion.4), channel_id=1, source_target_pairs={{0,1},{1,2},{2,3},{3,4},{4,5},{5,6},{6,7},{7,8},{8,9},{9,10},{10,1... | collective-permute-start | bytes 663560 | tf_op jit(solution)/shard_map/ppermute | solution.py:18
  (31 other events, 141.6 us)
Sparse Core Ops, SparseCore 0:
  466.3 79.3 all-gather.1
where the time goes:
time: 700 us; the launch traced here: 694 us
  local copies, waits for them, and re-layouts  172 us (25%)
  blocking collectives  169 us (24%)
  other arithmetic  165 us (24%)
  matrix products  118 us (17%)
  waiting for transfers between devices  34.2 us (5%)
  starting transfers between devices  19.9 us (3%)
  between operations  15.4 us (2%)
    scatter-add x1, other arithmetic, attend(): scores = scores + jnp.take(bias_table, bias_index, axis=1)[None]  112 us
    all_to_all x1, blocking collectives, sent_and_summed(): lax.all_to_all(blocks, axis, split_axis=0, concat_axis=0, tiled=True)  84.6 us
    psum x1, blocking collectives, per_device(): table_grad = lax.psum(grad_table, ('lat', 'lon')) * factor  65.4 us
    gather x2, local copies, waits for them, and re-layouts, attend(): scores = scores + jnp.take(bias_table, bias_index, axis=1)[None]  50.9 us
    dot_general x3, matrix products, attend(): jnp.einsum('whij,wjhd->wihd', probability, valued, precision=precise)  30 us
    dot_general x3, matrix products, attend(): jnp.einsum('wihd,wjhd->whij', query, keyed, precision=precise)  22.1 us
    dot_general x3, matrix products, attend(): jnp.dot(flat_rows, w_qkv, precision=precise, preferred_element_type=jnp.f...  21.5 us
    all_to_all x1, blocking collectives, copy_for_each(): return lax.all_to_all(copies, axis, split_axis=0, concat_axis=0, tiled=True)  19.5 us
  transfers between devices with their start and end apart: 10, of which 3 were waited for; matrix products, arithmetic and copies ran while one was open for 35% of the time, Pallas kernels for 0%

commit v1 on v0

--- a/solution.py
+++ b/solution.py
@@ -164,7 +164,7 @@
     own_new = own_weights - 0.01 * first_new / (jnp.sqrt(second_new) + 1e-08)
     along_lon = collect(own_new, "lon", 0)
     gathered = lax.all_gather(along_lon, "lat", axis=0, tiled=True)
-    table_grad = lax.psum(grad_table, ("lat", "lon")) * factor
+    table_grad = jnp.sum(lax.all_gather(grad_table, ("lat", "lon")), axis=0) * factor
     return (grad_input, gathered, first_new, second_new, table_grad)
 
 

time: 700 us -> 767 us (1.096)
  waiting for transfers between devices: 34.2 us -> 252 us
  blocking collectives: 169 us -> 20.2 us
    all_gather x0 -> x1, waiting for transfers between devices: none -> 130 us  [per_device(): lax.all_gather(grad_table, ('lat', 'lon'))]
    all_to_all x1 -> x0, blocking collectives: 84.6 us -> none  [sent_and_summed(): lax.all_to_all(blocks, axis, split_axis=0, concat_axis=0, tiled=True)]
    all_gather x1, waiting for transfers between devices: 0.01 us -> 76.7 us  [per_device(): gathered = lax.all_gather(along_lon, 'lat', axis=0, tiled=True)]
    psum x1 -> x0, blocking collectives: 65.4 us -> none  [per_device(): table_grad = lax.psum(grad_table, ('lat', 'lon')) * factor]
    ppermute x8, waiting for transfers between devices: 18.1 us -> 28.8 us  [passed_along(): lax.ppermute(value, axis, [(i, (i + by) % size) for i in range(size)])]
    all_to_all x1 -> x2, waiting for transfers between devices: 16.1 us -> 16.7 us  [sent_and_summed(): lax.all_to_all(blocks, axis, split_axis=0, concat_axis=0, tiled=True)]
  transfers between devices with their start and end apart: 10 -> 12, of which waited for: 3 -> 6; matrix products, arithmetic and copies ran while one was open for 35% -> 34% of each run, Pallas kernels for 0% -> 0%
where the time goes in v1:
time: 767 us; the launch traced here: 761 us
  waiting for transfers between devices  252 us (33%)
  local copies, waits for them, and re-layouts  170 us (22%)
  other arithmetic  164 us (21%)
  matrix products  115 us (15%)
  starting transfers between devices  24.4 us (3%)
  blocking collectives  20.2 us (3%)
  between operations  15.4 us (2%)
    all_gather x1, waiting for transfers between devices, per_device(): lax.all_gather(grad_table, ('lat', 'lon'))  130 us
    scatter-add x1, other arithmetic, attend(): scores = scores + jnp.take(bias_table, bias_index, axis=1)[None]  112 us
    all_gather x1, waiting for transfers between devices, per_device(): gathered = lax.all_gather(along_lon, 'lat', axis=0, tiled=True)  76.7 us
    gather x2, local copies, waits for them, and re-layouts, attend(): scores = scores + jnp.take(bias_table, bias_index, axis=1)[None]  50.7 us
    dot_general x3, matrix products, attend(): jnp.einsum('whij,wjhd->wihd', probability, valued, precision=precise)  30.1 us
    ppermute x8, waiting for transfers between devices, passed_along(): lax.ppermute(value, axis, [(i, (i + by) % size) for i in range(size)])  28.8 us
    dot_general x3, matrix products, attend(): jnp.einsum('wihd,wjhd->whij', query, keyed, precision=precise)  22.4 us
    dot_general x3, matrix products, attend(): jnp.dot(flat_rows, w_qkv, precision=precise, preferred_element_type=jnp.f...  21.2 us
  transfers between devices with their start and end apart: 12, of which 6 were waited for; matrix products, arithmetic and copies ran while one was open for 34% of the time, Pallas kernels for 0%

profile of v1, /device:TPU:0, one launch (start us, length us, event | category | flops | bytes accessed | tf_op | source)
XLA Modules:
  0.0 761.1 jit_solution(9953034843579919038)
XLA Ops:
  8.9 6.2 collective-permute-start
  20.4 38.7 %gather_fusion = f32[20736,12]{1,0:T(8,128)} fusion(f32[12,529]{0,1:T(8,128)S(1)} %copy.133, s32[21504]{0:T(1024)S(1)} %pad_clamp_fusion), kind=kCustom, calls=%fused_computation | custom fusion | bytes 2073600 | tf_op jit(solution)/shard_map/jvp(jit(_take))/gather | solution.py:88
  59.0 12.1 %copy.134 = f32[144,144,12]{0,1,2:T(8,128)} copy(f32[144,144,12]{2,1,0:T(8,128)} %bitcast.116) | data formatting | bytes 1990656 | tf_op jit(solution)/shard_map/jvp(jit(_take))/gather | solution.py:88
  92.6 7.9 %convolution_bitcast_fusion = f32[2,2,12,12,1152]{4,3,1,2,0:T(8,128)S(1)} fusion(f32[384,1152,1,1,1]{1,0,2,3,4:T(8,128)} %reshape.396, f32[2,12,2,12,384]{4,3,2,1,0:T(8,128)} %squeeze.11, f32[2,12,2,12]{3,2,1,0:T(2,128)} %sqrt.38, f32[2,12,2,12]{3,2,1,0:T(2,128)} %div.137), kind=kOutput, calls=%fused_computation.14 | convolution fusion | flops 3058089984 | bytes 5313024 | tf_op jit(solution)/shard_map/jvp()/dot_general | solution.py:81
  118.9 9.7 %fusion.4 = (f32[4,12,144]{2,1,0:T(8,128)S(1)}, f32[4,12,144,144]{2,3,1,0:T(8,128)S(1)}) fusion(f32[12,144,144]{1,2,0:T(8,128)S(1)} %select_bitcast_fusion, pred[4,144,144]{1,2,0:T(8,128)(4,1)S(1)} %copy-done.24, f32[4,144,12,32]{1,3,2,0:T(8,128)} %bitcast.119, f32[4,144,12,32]{1,3,2,0:T(8,128)} %bitcast.117), kind=kOutput, calls=%fused_computation.11 | convolution fusion | flops 386180352 | bytes 6856704 | tf_op jit(solution)/shard_map/jvp(wihd,wjhd->whij)/dot_general | solution.py:87
  131.5 7.1 fusion.25
  138.7 6.1 copy.136
  168.2 9.1 %collective-permute-done.3 = f32[1,24,6,384]{3,2,1,0:T(8,128)S(1)} collective-permute-done((f32[1,24,6,384]{3,2,1,0:T(8,128)S(1)}, f32[1,24,6,384]{3,2,1,0:T(8,128)S(1)}, u32[]{:S(2)}, u32[]{:S(2)}) %collective-permute-start.3) | collective-permute-done | bytes 221216 | tf_op jit(solution)/shard_map/ppermute | solution.py:18
  178.1 5.7 fusion.59
  183.9 7.7 %fusion.10 = f32[576,1536]{1,0:T(8,128)S(1)} fusion(f32[576,1536]{1,0:T(8,128)S(1)} %fusion.59, f32[576,384]{1,0:T(8,128)S(1)} %bitcast.135, f32[1536,384]{1,0:T(8,128)S(1)} %copy-done.30), kind=kOutput, calls=%fused_computation.20 | convolution fusion | flops 4093673472 | bytes 10321920 | tf_op jit(solution)/shard_map/transpose(jvp())/dot_general | solution.py:115
  191.6 5.8 multiply_reduce_fusion.2
  198.8 9.7 %fusion.11 = f32[1536,384]{1,0:T(8,128)} fusion(f32[576,384]{1,0:T(8,128)S(1)} %bitcast.136, f32[576,1536]{1,0:T(8,128)S(1)} %fusion.59), kind=kOutput, calls=%fused_computation.21 | convolution fusion | flops 4083941376 | bytes 6782976 | tf_op jit(solution)/shard_map/transpose(jvp())/dot_general | solution.py:115
  214.0 5.9 fusion.60
  232.6 5.7 copy.139
  238.3 13.7 %fusion.17 = f32[4,12,32,144]{3,2,1,0:T(8,128)} fusion(f32[4,12,32,144]{3,2,1,0:T(8,128)} %copy.139, f32[4,12,144]{2,1,0:T(8,128)} %copy-done.39, f32[4,12,144,144]{2,3,1,0:T(8,128)} %copy-done, f32[4,12,144]{2,1,0:T(8,128)} %copy-done.35, f32[12,144,144]{1,2,0:T(8,128)} %copy-done.1, pred[4,144,144]{1,2,0:T(8,128)(4,1)} %compare_and_fusion), kind=kOutput, calls=%fused_computation.28 | convolution fusion | flops 387182592 | bytes 6884352 | tf_op jit(solution)/shard_map/transpose(jvp(whij,wjhd->wihd))/dot_general | solution.py:101
  252.2 9.3 %multiply_reduce_fusion = (f32[4,12,144]{2,1,0:T(8,128)S(1)}, f32[4,12,144,144]{2,3,1,0:T(8,128)S(1)}) fusion(f32[4,12,144]{2,1,0:T(8,128)S(1)} %copy-done.44, f32[4,12,144]{2,1,0:T(8,128)S(1)} %copy-done.36, f32[12,144,144]{1,2,0:T(8,128)S(1)} %copy-done.2, f32[4,12,144,144]{2,3,1,0:T(8,128)S(1)} %bitcast.113, pred[4,144,144]{1,2,0:T(8,128)(4,1)S(1)} %copy-done.25, ...), kind=kOutput, calls=%fused_computation.4 | convolution fusion | flops 389166336 | bytes 10893312 | tf_op jit(solution)/shard_map/transpose(jvp(whij,wjhd->wihd))/dot_general | solution.py:101
  261.5 5.1 fusion.53
  270.8 8.6 %fusion.2 = f32[4,12,144,32]{2,3,1,0:T(8,128)} fusion(f32[4,144,12,32]{1,3,2,0:T(8,128)S(1)} %bitcast.120, f32[4,12,144,144]{2,3,1,0:T(8,128)S(1)} %get-tuple-element.26), kind=kOutput, calls=%fused_computation.9 | convolution fusion | flops 383201280 | bytes 5750784 | tf_op jit(solution)/shard_map/transpose(jvp(wihd,wjhd->whij))/dot_general | solution.py:87
  301.4 7.1 fusion.62
  311.1 11.5 %add_add_fusion = f32[1769472]{0:T(1024)} fusion(f32[442368]{0:T(1024)} %reshape.370, f32[147456]{0:T(1024)} %reshape.368, f32[589824]{0:T(1024)} %reshape.366, f32[589824]{0:T(1024)S(1)} %copy-done.8), kind=kLoop, calls=%fused_computation.2 | loop fusion | flops 5308416 | bytes 14155776 | tf_op jit(solution)/shard_map/add | solution.py:155
  322.7 5.1 all-to-all-start
  327.9 10.4 %copy.163 = f32[144,144,12]{2,1,0:T(8,128)} copy(f32[144,144,12]{0,1,2:T(8,128)S(1)} %bitcast.127) | data formatting | bytes 1990656 | tf_op jit(solution)/shard_map/transpose(jvp())/reduce_sum | solution.py:88
  338.2 112.4 %scatter_custom_fusion = f32[12,529]{0,1:T(8,128)S(1)} fusion(s32[20736]{0:T(1024)} %copy-done.41, f32[20736,12]{1,0:T(8,128)} %bitcast.122, f32[]{:T(128)} %constant.31.clone.1), kind=kCustom, calls=%fused_computation.81 | custom fusion | flops 248832 | bytes 25904 | tf_op jit(solution)/shard_map/transpose(jvp(jit(_take)))/scatter-add | solution.py:88
  451.5 10.5 %reduce_sum.160 = f32[221184]{0:T(1024)} reduce(f32[8,1,221184]{2,1,0:T(1,128)} %all-to-all-done, f32[]{:T(128)} %constant.31.clone.1), dimensions={0,1}, to_apply=%region_11.12 | reduce | flops 1548288 | bytes 7962628 | tf_op jit(solution)/shard_map/reduce_sum | solution.py:29
  465.9 16.7 %all-to-all-done.1 = f32[16,1,13824]{2,1,0:T(1,128)S(1)} async-done(((f32[16,1,13824]{2,1,0:T(1,128)}), f32[16,1,13824]{2,1,0:T(1,128)S(1)}, u32[]{:S(2)}, u32[]{:S(2)}) %all-to-all-start.1) | async-done | bytes 884768 | tf_op jit(solution)/shard_map/all_to_all | solution.py:28
  485.1 20.2 %all_to_all.24 = f32[16,1,13824]{2,1,0:T(1,128)} all-to-all(f32[16,1,13824]{2,1,0:T(1,128)S(1)} %broadcast_in_dim.93), channel_id=1, replica_groups=mesh['lat'=8,'lon'=16] {'lon'}, dimensions={0} | all-to-all | bytes 1769472 | tf_op jit(solution)/shard_map/all_to_all | solution.py:40
  509.7 6.2 multiply_reduce_fusion.1
  517.8 9.8 %collective-permute-done.6 = f32[1,6,24,384]{3,2,1,0:T(8,128)S(1)} collective-permute-done((f32[1,6,24,384]{3,2,1,0:T(8,128)S(1)}, f32[1,6,24,384]{3,2,1,0:T(8,128)S(1)}, u32[]{:S(2)}, u32[]{:S(2)}) %collective-permute-start.6) | collective-permute-done | bytes 221216 | tf_op jit(solution)/shard_map/ppermute | solution.py:18
  527.7 9.9 %collective-permute-done.7 = f32[1,24,6,384]{3,2,1,0:T(8,128)S(1)} collective-permute-done((f32[1,24,6,384]{3,2,1,0:T(8,128)S(1)}, f32[1,24,6,384]{3,2,1,0:T(8,128)S(1)}, u32[]{:S(2)}, u32[]{:S(2)}) %collective-permute-start.7) | collective-permute-done | bytes 221216 | tf_op jit(solution)/shard_map/ppermute | solution.py:18
  538.8 129.6 %all-gather.7.cloned.1.call-done = f32[128,12,529]{2,1,0:T(8,128)} async-done(((f32[1,12,529]{2,1,0:T(8,128)}), f32[128,12,529]{2,1,0:T(8,128)}) %all-gather.7.cloned.1.call-update) | async-done | bytes 3250192 | tf_op jit(solution)/shard_map/all_gather | solution.py:167
  672.2 76.7 %all-gather.5.cloned.1.call-done = f32[1769472]{0:T(1024)} async-done(((f32[221184]{0:T(1024)}), f32[1769472]{0:T(1024)}) %all-gather.5.cloned.1.call-update) | async-done | bytes 7077904 | tf_op jit(solution)/shard_map/all_gather | solution.py:166
  748.8 5.2 copy.171
  (228 shorter events, 140.6 us)
Async XLA Ops:
  7.2 13.0 %copy-start.51 = (f32[12,529]{1,0:T(8,128)S(1)}, f32[12,529]{1,0:T(8,128)}, u32[]{:S(2)}) copy-start(f32[12,529]{1,0:T(8,128)} %param.13) | copy-start | bytes 76180
  8.9 63.9 %collective-permute-start = (f32[1,24,6,384]{3,2,1,0:T(8,128)}, f32[1,24,6,384]{3,2,1,0:T(8,128)S(1)}, u32[]{:S(2)}, u32[]{:S(2)}) collective-permute-start(f32[1,24,6,384]{3,2,1,0:T(8,128)} %slice.139), channel_id=1, source_target_pairs={{0,15},{1,0},{2,1},{3,2},{4,3},{5,4},{6,5},{7,6},{8,7},{9,8},{10,9... | collective-permute-start | bytes 663560 | tf_op jit(solution)/shard_map/ppermute | solution.py:18
  72.8 58.1 %copy-start.1 = (f32[12,144,144]{1,2,0:T(8,128)}, f32[12,144,144]{1,2,0:T(8,128)S(1)}, u32[]{:S(2)}) copy-start(f32[12,144,144]{1,2,0:T(8,128)S(1)} %select_bitcast_fusion) | copy-start | bytes 2985988
  73.6 12.9 %collective-permute-start.1 = (f32[1,6,24,384]{3,2,1,0:T(8,128)}, f32[1,6,24,384]{3,2,1,0:T(8,128)S(1)}, u32[]{:S(2)}, u32[]{:S(2)}) collective-permute-start(f32[1,6,24,384]{3,2,1,0:T(8,128)} %pad_maximum_fusion.7), channel_id=1, source_target_pairs={{0,112},{16,0},{32,16},{48,32},{64,48},{80,64},{96,80},{112,96},{1... | collective-permute-start | bytes 663560 | tf_op jit(solution)/shard_map/ppermute | solution.py:18
  86.5 14.0 %copy-start.16 = (f32[1,6,24,384]{3,2,1,0:T(8,128)}, f32[1,6,24,384]{3,2,1,0:T(8,128)S(1)}, u32[]{:S(2)}) copy-start(f32[1,6,24,384]{3,2,1,0:T(8,128)S(1)} %collective-permute-done.1) | copy-start | bytes 663556
  86.7 13.8 %copy-start.37 = (f32[24,24]{1,0:T(8,128)}, f32[24,24]{1,0:T(8,128)S(1)}, u32[]{:S(2)}) copy-start(f32[24,24]{1,0:T(8,128)S(1)} %broadcast_multiply_fusion.2) | copy-start | bytes 6916
  130.8 36.8 %copy-start.39 = (f32[4,12,144]{2,1,0:T(8,128)}, f32[4,12,144]{2,1,0:T(8,128)S(1)}, u32[]{:S(2)}) copy-start(f32[4,12,144]{2,1,0:T(8,128)S(1)} %fusion.52) | copy-start | bytes 82948
  152.0 15.1 %collective-permute-start.2 = (f32[1,6,24,384]{3,2,1,0:T(8,128)}, f32[1,6,24,384]{3,2,1,0:T(8,128)S(1)}, u32[]{:S(2)}, u32[]{:S(2)}) collective-permute-start(f32[1,6,24,384]{3,2,1,0:T(8,128)} %slice.145), channel_id=1, source_target_pairs={{0,16},{16,32},{32,48},{48,64},{64,80},{80,96},{96,112},{112,0},{1... | collective-permute-start | bytes 663560 | tf_op jit(solution)/shard_map/ppermute | solution.py:18
  161.3 16.0 %copy-start.23 = (f32[24,24,384]{2,1,0:T(8,128)S(1)}, f32[24,24,384]{2,1,0:T(8,128)}, u32[]{:S(2)}) copy-start(f32[24,24,384]{2,1,0:T(8,128)} %param.8) | copy-start | bytes 2654212
  167.1 10.2 %collective-permute-start.3 = (f32[1,24,6,384]{3,2,1,0:T(8,128)S(1)}, f32[1,24,6,384]{3,2,1,0:T(8,128)S(1)}, u32[]{:S(2)}, u32[]{:S(2)}) collective-permute-start(f32[1,24,6,384]{3,2,1,0:T(8,128)S(1)} %pad_maximum_fusion.5), channel_id=1, source_target_pairs={{0,1},{1,2},{2,3},{3,4},{4,5},{5,6},{6,7},{7,8},{8,9},{9,10},{10,1... | collective-permute-start | bytes 663560 | tf_op jit(solution)/shard_map/ppermute | solution.py:18
  198.5 10.0 %collective-permute-start.4 = (f32[1,24,6,384]{3,2,1,0:T(8,128)S(1)}, f32[1,24,6,384]{3,2,1,0:T(8,128)S(1)}, u32[]{:S(2)}, u32[]{:S(2)}) collective-permute-start(f32[1,24,6,384]{3,2,1,0:T(8,128)S(1)} %slice.148), channel_id=1, source_target_pairs={{0,15},{1,0},{2,1},{3,2},{4,3},{5,4},{6,5},{7,6},{8,7},{9,8},{10,9... | collective-permute-start | bytes 663560 | tf_op jit(solution)/shard_map/ppermute | solution.py:18
  209.5 16.5 %collective-permute-start.5 = (f32[1,6,24,384]{3,2,1,0:T(8,128)}, f32[1,6,24,384]{3,2,1,0:T(8,128)S(1)}, u32[]{:S(2)}, u32[]{:S(2)}) collective-permute-start(f32[1,6,24,384]{3,2,1,0:T(8,128)} %pad_maximum_fusion.6), channel_id=1, source_target_pairs={{0,112},{16,0},{32,16},{48,32},{64,48},{80,64},{96,80},{112,96},{1... | collective-permute-start | bytes 663560 | tf_op jit(solution)/shard_map/ppermute | solution.py:18
  232.6 19.5 %slice-start = ((s8[7077888]{0:T(1024)(128)(4,1)}), s8[2883584]{0:T(1024)(128)(4,1)S(1)}, s32[]{:S(2)}) async-start(s8[7077888]{0:T(1024)(128)(4,1)} %bitcast.112), calls=%async_computation.5 | async-start | bytes 5767168
  238.3 13.8 %slice-start.1 = ((s8[7077888]{0:T(1024)(128)(4,1)}), s8[4194304]{0:T(1024)(128)(4,1)S(1)}, s32[]{:S(2)}) async-start(s8[7077888]{0:T(1024)(128)(4,1)} %bitcast.112), calls=%async_computation.6 | async-start | bytes 8388608
  238.3 13.8 %copy-start.2 = (f32[12,144,144]{1,2,0:T(8,128)S(1)}, f32[12,144,144]{1,2,0:T(8,128)}, u32[]{:S(2)}) copy-start(f32[12,144,144]{1,2,0:T(8,128)} %copy-done.1) | copy-start | bytes 2985988
  238.3 13.8 %copy-start.20 = (f32[4,144,384]{1,2,0:T(8,128)S(1)}, f32[4,144,384]{1,2,0:T(8,128)}, u32[]{:S(2)}) copy-start(f32[4,144,384]{1,2,0:T(8,128)} %copy.128) | copy-start | bytes 2654212
  238.3 13.8 %copy-start.21 = (f32[4,12,32,144]{3,2,1,0:T(8,128)S(1)}, f32[4,12,32,144]{3,2,1,0:T(8,128)}, u32[]{:S(2)}) copy-start(f32[4,12,32,144]{3,2,1,0:T(8,128)} %copy.139) | copy-start | bytes 2654212
  238.3 13.8 %copy-start.25 = (pred[4,144,144]{1,2,0:T(8,128)(4,1)S(1)}, pred[4,144,144]{1,2,0:T(8,128)(4,1)}, u32[]{:S(2)}) copy-start(pred[4,144,144]{1,2,0:T(8,128)(4,1)} %compare_and_fusion) | copy-start | bytes 248836
  238.3 13.8 %copy-start.36 = (f32[4,12,144]{2,1,0:T(8,128)S(1)}, f32[4,12,144]{2,1,0:T(8,128)}, u32[]{:S(2)}) copy-start(f32[4,12,144]{2,1,0:T(8,128)} %copy-done.35) | copy-start | bytes 82948
  238.3 13.8 %copy-start.44 = (f32[4,12,144]{2,1,0:T(8,128)S(1)}, f32[4,12,144]{2,1,0:T(8,128)}, u32[]{:S(2)}) copy-start(f32[4,12,144]{2,1,0:T(8,128)} %multiply_divide_fusion) | copy-start | bytes 82948
  322.7 128.9 %all-to-all-start = ((f32[8,1,221184]{2,1,0:T(1,128)}), f32[8,1,221184]{2,1,0:T(1,128)}, u32[]{:S(2)}, u32[]{:S(2)}) async-start(f32[8,1,221184]{2,1,0:T(1,128)} %bitcast.114), calls=%async_computation | async-start | bytes 14155776 | tf_op jit(solution)/shard_map/all_to_all | solution.py:28
  327.8 340.6 %all-gather.7.cloned.1.call-start = ((), (), s32[]{:S(2)}) async-start(), calls=%async_computation.4 | async-start | bytes 5283840 | tf_op jit(solution)/shard_map/all_gather | solution.py:167
  451.5 31.6 %copy-start.49 = (f32[13824]{0:T(1024)S(1)}, f32[13824]{0:T(1024)}, u32[]{:S(2)}) copy-start(f32[13824]{0:T(1024)} %param.11) | copy-start | bytes 165892
  451.5 31.6 %copy-start.50 = (f32[13824]{0:T(1024)S(1)}, f32[13824]{0:T(1024)}, u32[]{:S(2)}) copy-start(f32[13824]{0:T(1024)} %param.12) | copy-start | bytes 165892
  462.0 43.2 %copy-start.3 = (f32[442368]{0:T(1024)S(1)}, f32[442368]{0:T(1024)}, u32[]{:S(2)}) copy-start(f32[442368]{0:T(1024)} %slice.115) | copy-start | bytes 5308420
  462.0 20.5 %all-to-all-start.1 = ((f32[16,1,13824]{2,1,0:T(1,128)}), f32[16,1,13824]{2,1,0:T(1,128)S(1)}, u32[]{:S(2)}, u32[]{:S(2)}) async-start(f32[16,1,13824]{2,1,0:T(1,128)} %bitcast.137), calls=%async_computation.1 | async-start | bytes 1769472 | tf_op jit(solution)/shard_map/all_to_all | solution.py:28
  465.8 283.0 %all-gather.5.cloned.1.call-start = ((), (), s32[]{:S(2)}) async-start(), calls=%async_computation.3 | async-start | bytes 7962624 | tf_op jit(solution)/shard_map/all_gather | solution.py:166
  515.9 21.7 %copy-start.15 = (f32[24,24,384]{2,1,0:T(8,128)S(1)}, f32[24,24,384]{2,1,0:T(8,128)}, u32[]{:S(2)}) copy-start(f32[24,24,384]{2,1,0:T(8,128)} %copy-done.14) | copy-start | bytes 2654212
  515.9 21.7 %copy-start.29 = (f32[24,24,384]{2,1,0:T(8,128)S(1)}, f32[24,24,384]{2,1,0:T(8,128)}, u32[]{:S(2)}) copy-start(f32[24,24,384]{2,1,0:T(8,128)} %param.9) | copy-start | bytes 2654212
  515.9 21.6 %copy-start.46 = (f32[24,24]{1,0:T(8,128)S(1)}, f32[24,24]{1,0:T(8,128)}, u32[]{:S(2)}) copy-start(f32[24,24]{1,0:T(8,128)} %copy-done.45) | copy-start | bytes 6916
  516.8 10.8 %collective-permute-start.6 = (f32[1,6,24,384]{3,2,1,0:T(8,128)S(1)}, f32[1,6,24,384]{3,2,1,0:T(8,128)S(1)}, u32[]{:S(2)}, u32[]{:S(2)}) collective-permute-start(f32[1,6,24,384]{3,2,1,0:T(8,128)S(1)} %slice.151), channel_id=1, source_target_pairs={{0,16},{16,32},{32,48},{48,64},{64,80},{80,96},{96,112},{112,0},{1... | collective-permute-start | bytes 663560 | tf_op jit(solution)/shard_map/ppermute | solution.py:18
  527.6 9.9 %collective-permute-start.7 = (f32[1,24,6,384]{3,2,1,0:T(8,128)S(1)}, f32[1,24,6,384]{3,2,1,0:T(8,128)S(1)}, u32[]{:S(2)}, u32[]{:S(2)}) collective-permute-start(f32[1,24,6,384]{3,2,1,0:T(8,128)S(1)} %pad_maximum_fusion.4), channel_id=1, source_target_pairs={{0,1},{1,2},{2,3},{3,4},{4,5},{5,6},{6,7},{7,8},{8,9},{9,10},{10,1... | collective-permute-start | bytes 663560 | tf_op jit(solution)/shard_map/ppermute | solution.py:18
  (34 other events, 145.2 us)
Sparse Core Ops, SparseCore 0:
  451.6 216.7 all-gather.6
  670.0 78.7 all-gather.4
